TPU v7x, 256 devices: a whole 4x4x8 slice. The times are simulated.
256 devices in a mesh: row: 8 (over z), col: 32 (over x, y, core).
Axes of the slice: x: 4, y: 4, z: 8, core: 2. Of those that a mesh axis runs over, the one named last changes fastest.
Arguments:
- latitude: bfloat16 [16384, 256], P(('row', 'col')), may hold values from -4 to 4
- longitude: bfloat16 [16384, 512], P(('row', 'col')), may hold values from -4 to 4
- weight: bfloat16 [16384], P(('row', 'col')), may hold values from 0.29882812 to 3
- harmonic_index: int32 [2, 24576], P(None, 'col'), may hold values from 0 to 511, as said below
Outputs:
- coefficients: float32 [512, 24576], P(None, 'col')
- residual: float32 [16384, 24576], P('row', 'col')
Inputs may be any that keep to these rules, and one draw needn't show every extreme that they name: The pairs (harmonic_index[0, j], harmonic_index[1, j]) are distinct over all 24576 columns; row 0 is below 256, and harmonic_index[1, j] // 2 never exceeds harmonic_index[0, j].
All inputs are finite; a program needn't handle non-finite values.
Results may differ from a plain program's by a relative error of at most 0.0003.
Values may be sent and summed in bfloat16 or wider, within the bound.
No kernel may reach another device: no remote copies, remote signals or barrier semaphores. Data moves between devices by JAX's collectives and lax.ppermute only.
A program may use at most 128 MiB of HBM per device.

v0:
```python
import math
import jax
import jax.numpy as jnp
from jax import lax
from jax.sharding import PartitionSpec as P

PANEL = 256


def in_one_piece(arrays, axis, dim, along):
    widths = [math.prod(a.shape[along:]) for a in arrays]
    both = jnp.concatenate(
        [a.reshape(*a.shape[:along], w) for a, w in zip(arrays, widths)], axis=along
    )
    result = lax.all_gather(both, axis, axis=dim, tiled=True)
    tiles = jnp.split(result, [sum(widths[:k]) for k in range(1, len(widths))], axis=along)
    return tuple(
        (b.reshape(*result.shape[:along], *a.shape[along:]) for a, b in zip(arrays, tiles))
    )


def picked(array, axis, root):
    return lax.dynamic_index_in_dim(lax.all_gather(array, axis), root, 0, keepdims=False)


def synthesize(latitude, longitude, weight, column_index):
    degree_hot = (
        column_index[0][None, :] == jnp.arange(latitude.shape[1], dtype=jnp.int32)[:, None]
    ).astype(jnp.bfloat16)
    order_hot = (
        column_index[1][None, :] == jnp.arange(longitude.shape[1], dtype=jnp.int32)[:, None]
    ).astype(jnp.bfloat16)
    picked_degree = jnp.dot(latitude, degree_hot, preferred_element_type=jnp.float32)
    picked_order = jnp.dot(longitude, order_hot, preferred_element_type=jnp.float32)
    return weight.astype(jnp.float32)[:, None] * picked_degree * picked_order


def orthonormal(panel_cols, gram_sum):
    lower_factor = jnp.linalg.cholesky(gram_sum)
    return lax.linalg.triangular_solve(lower_factor, panel_cols.T, left_side=True, lower=True)


def remove_span(design, basis_t, top_rows):
    return design - jnp.dot(
        basis_t.T, top_rows, precision=lax.Precision.HIGHEST, preferred_element_type=jnp.float32
    )


def shards(latitude, longitude, weight, harmonic_index):
    tables = in_one_piece((latitude, longitude, weight), "col", 0, 1)
    lead_index = picked(harmonic_index[:, : 2 * PANEL], "col", 0)
    lead_cols = synthesize(tables[0], tables[1], tables[2], lead_index)
    design = synthesize(tables[0], tables[1], tables[2], harmonic_index)
    local_gram = jnp.dot(
        lead_cols.T, lead_cols, precision=lax.Precision.HIGHEST, preferred_element_type=jnp.float32
    )
    gram_sum = lax.psum(local_gram, "row")
    basis_t = orthonormal(lead_cols, gram_sum)
    local_rows = jnp.dot(
        basis_t, design, precision=lax.Precision.HIGHEST, preferred_element_type=jnp.float32
    )
    coefficients = lax.psum(local_rows, "row")
    residual = remove_span(design, basis_t, coefficients)
    return (coefficients, residual)


def solution(mesh):
    return jax.shard_map(
        shards,
        mesh=mesh,
        in_specs=(
            P(("row", "col"), None),
            P(("row", "col"), None),
            P(("row", "col")),
            P(None, "col"),
        ),
        out_specs=(P(None, "col"), P("row", "col")),
        check_vma=False,
    )
```

profile of v0, /device:TPU:2, one launch (start us, length us, event | category | flops | bytes accessed | tf_op | source)
XLA Modules:
  0.0 433.0 jit_solution(3629395771598168058)
XLA Ops:
  7.2 0.8 copy.12
  8.0 1.5 pad_maximum_fusion.3
  9.5 0.7 slice_bitcast_fusion.8
  10.2 24.6 %all-gather.1 = s32[32,2,512]{2,1,0:T(2,128)S(1)} all-gather(s32[1,2,512]{2,1,0:T(2,128)S(1)} %slice_bitcast_fusion.8), channel_id=2, replica_groups=mesh['row'=8,'col'=32] {'col'}, dimensions={0}, use_global_device_ids=true | all-gather | bytes 135168 | tf_op jit(solution)/shard_map/all_gather | solution.py:23
  34.8 0.8 slice_reduce_fusion
  35.6 28.7 %all-gather.4.cloned.1.call-done = bf16[2048,769]{1,0:T(8,128)(2,1)} async-done(((bf16[64,769]{1,0:T(8,128)(2,1)}), bf16[2048,769]{1,0:T(8,128)(2,1)}) %all-gather.4.cloned.1.call-update) | async-done | bytes 3149840 | tf_op jit(solution)/shard_map/all_gather | solution.py:15
  64.3 1.4 convert_reduce_fusion
  65.7 2.0 fusion.20
  67.7 1.3 multiply_multiply_fusion.1
  69.0 1.9 copy-done
  70.9 8.0 %fusion.49 = f32[512,512]{0,1:T(8,128)} fusion(f32[2048,512]{1,0:T(8,128)S(1)} %multiply_multiply_fusion.1), kind=kOutput, calls=%fused_computation.94 | convolution fusion | flops 6442450944 | bytes 5242880 | tf_op jit(solution)/shard_map/dot_general | solution.py:54
  79.3 2.4 fusion.18
  81.7 4.7 %multiply_multiply_fusion = f32[2048,768]{1,0:T(8,128)} fusion(f32[2048,768]{1,0:T(8,128)S(1)} %fusion.18, f32[2048]{0:T(1024)S(1)} %convert_reduce_fusion, bf16[2048,769]{1,0:T(8,128)(2,1)S(1)} %copy-done.3, s32[768]{0:T(1024)S(1)} %get-tuple-element.10), kind=kOutput, calls=%fused_computation.2 | convolution fusion | flops 1614151680 | bytes 14692352 | tf_op jit(solution)/shard_map/dot_general | solution.py:34
  86.4 68.5 %all-reduce.4.cloned.1.call-done = f32[512,512]{0,1:T(8,128)} async-done(((f32[512,512]{0,1:T(8,128)}), f32[512,512]{0,1:T(8,128)}) %all-reduce.4.cloned.1.call-update) | async-done | bytes 1048592 | tf_op jit(solution)/shard_map/psum | solution.py:57
  154.9 1.6 copy.14
  156.4 1.4 fusion.17
  157.9 11.7 %cholesky.104 = f32[128,128]{1,0:T(8,128)S(1)} custom-call(f32[128,128]{1,0:T(8,128)S(1)} %cholesky.266), custom_call_target="Cholesky" | custom-call | tf_op jit(solution)/shard_map/jit(cholesky)/cholesky | solution.py:39
  169.6 9.8 %custom-call.30 = f32[1,128,128]{1,2,0:T(8,128)S(1)} custom-call(f32[1,128,128]{2,1,0:T(8,128)S(1)} %get-tuple-element.33), custom_call_target="InvertDiagBlocksLowerTriangular" | custom-call | tf_op jit(solution)/shard_map/jit(cholesky)/cholesky | solution.py:39
  180.3 12.2 %cholesky.217 = f32[128,128]{1,0:T(8,128)S(1)} custom-call(f32[128,128]{1,0:T(8,128)S(1)} %cholesky.270), custom_call_target="Cholesky" | custom-call | tf_op jit(solution)/shard_map/jit(cholesky)/cholesky | solution.py:39
  192.4 9.8 %custom-call.31 = f32[1,128,128]{1,2,0:T(8,128)S(1)} custom-call(f32[1,128,128]{2,1,0:T(8,128)S(1)} %get-tuple-element.30), custom_call_target="InvertDiagBlocksLowerTriangular" | custom-call | tf_op jit(solution)/shard_map/jit(cholesky)/cholesky | solution.py:39
  202.9 11.7 %cholesky.238 = f32[128,128]{1,0:T(8,128)S(1)} custom-call(f32[128,128]{1,0:T(8,128)S(1)} %cholesky.275), custom_call_target="Cholesky" | custom-call | tf_op jit(solution)/shard_map/jit(cholesky)/cholesky | solution.py:39
  214.7 0.7 compare_reduce_fusion.1
  215.3 9.8 %custom-call.32 = f32[1,128,128]{1,2,0:T(8,128)S(1)} custom-call(f32[1,128,128]{2,1,0:T(8,128)S(1)} %get-tuple-element.27), custom_call_target="InvertDiagBlocksLowerTriangular" | custom-call | tf_op jit(solution)/shard_map/jit(cholesky)/cholesky | solution.py:39
  225.7 11.9 %cholesky.255 = f32[128,128]{1,0:T(8,128)S(1)} custom-call(f32[128,128]{1,0:T(8,128)S(1)} %convolution_subtract_fusion.5), custom_call_target="Cholesky" | custom-call | tf_op jit(solution)/shard_map/jit(cholesky)/cholesky | solution.py:39
  237.6 0.7 compare_reduce_fusion
  238.3 0.7 compare_reduce_fusion.2
  241.7 10.3 %while.1 = (s32[]{:T(128)}, f32[512,512]{1,0:T(8,128)S(1)}, s32[4,2]{0,1:T(2,128)S(1)}, f32[4,128,128]{2,1,0:T(8,128)}, s32[]{:T(128)}) while((s32[]{:T(128)}, f32[512,512]{1,0:T(8,128)S(1)}, s32[4,2]{0,1:T(2,128)S(1)}, f32[4,128,128]{2,1,0:T(8,128)}, s32[]{:T(128)}) %tuple.33), condition=%wide.while_cond, body=%wide.while_body.sunk | while | flops 2 | bytes 132205 | solution.py:40
  241.8 0.5 fusion.60
  242.3 2.0 bitcast_dynamic-update-slice_fusion.2
  244.4 0.5 fusion.60
  244.9 2.0 bitcast_dynamic-update-slice_fusion.2
  247.0 0.5 fusion.60
  247.5 2.0 bitcast_dynamic-update-slice_fusion.2
  249.5 0.5 fusion.60
  250.1 2.0 bitcast_dynamic-update-slice_fusion.2
  252.0 40.2 %custom-call.33 = f32[4,128,128]{1,2,0:T(8,128)S(1)} custom-call(f32[4,128,128]{2,1,0:T(8,128)} %get-tuple-element.9), custom_call_target="InvertDiagBlocksLowerTriangular" | custom-call | tf_op jit(solution)/shard_map/triangular_solve | solution.py:40
  292.2 2.4 fusion.15
  294.7 3.0 convolution_subtract_fusion.2
  297.7 1.1 fusion.37
  298.8 3.5 convolution_subtract_fusion.1
  302.4 1.1 fusion.35
  303.5 6.6 %fusion.6 = f32[128,2048]{0,1:T(8,128)S(1)} fusion(f32[128,2048]{1,0:T(8,128)S(1)} %fusion.35, f32[128,2048]{1,0:T(8,128)S(1)} %fusion.37, f32[128,2048]{1,0:T(8,128)S(1)} %fusion.15, f32[512,2048]{0,1:T(8,128)S(1)} %bitcast.61, f32[512,512]{1,0:T(8,128)} %copy-done.6), kind=kOutput, calls=%fused_computation.12 | convolution fusion | flops 1209794560 | bytes 5439488 | tf_op jit(solution)/shard_map/triangular_solve | solution.py:40
  310.1 1.1 fusion.34
  311.2 1.0 copy-done.5
  312.2 11.6 %fusion.9 = f32[512,768]{1,0:T(8,128)} fusion(f32[2048,768]{1,0:T(8,128)S(1)} %bitcast.63, f32[128,2048]{1,0:T(8,128)S(1)} %fusion.34, f32[128,2048]{1,0:T(8,128)S(1)} %fusion.35, f32[128,2048]{1,0:T(8,128)S(1)} %fusion.37, f32[128,2048]{1,0:T(8,128)S(1)} %fusion.15), kind=kOutput, calls=%fused_computation.15 | convolution fusion | flops 9666822144 | bytes 12058624 | tf_op jit(solution)/shard_map/dot_general | solution.py:59
  323.8 77.3 %all-reduce.6.cloned.1.call-done = f32[512,768]{1,0:T(8,128)} async-done(((f32[512,768]{1,0:T(8,128)}), f32[512,768]{1,0:T(8,128)}) %all-reduce.6.cloned.1.call-update) | async-done | bytes 1572880 | tf_op jit(solution)/shard_map/psum | solution.py:62
  401.0 23.9 %convolution_subtract_fusion = f32[2048,768]{1,0:T(8,128)} fusion(f32[2048,768]{1,0:T(8,128)} %multiply_multiply_fusion, f32[512,768]{1,0:T(8,128)} %all-reduce.6.cloned.1.call-done, f32[128,2048]{1,0:T(8,128)} %copy-done.5, f32[128,2048]{1,0:T(8,128)S(1)} %fusion.35, f32[128,2048]{1,0:T(8,128)S(1)} %fusion.37, f32[128,2048]{1,0:T(8,128)S(1)} %fusion.15), kind=kOutput, calls=%fused_computation.5 | convolution fusion | flops 9668395008 | bytes 18350080 | tf_op jit(solution)/shard_map/dot_general | solution.py:44
  424.9 1.1 copy.39
  (46 shorter events, 3.0 us)
Async XLA Ops:
  7.2 57.1 %all-gather.4.cloned.1.call-start = ((), (), s32[]{:S(2)}) async-start(), calls=%async_computation | async-start | bytes 3784704 | tf_op jit(solution)/shard_map/all_gather | solution.py:15
  9.5 145.4 %all-reduce.4.cloned.1.call-start = ((), (), s32[]{:S(2)}) async-start(), calls=%async_computation.1 | async-start | bytes 2097152 | tf_op jit(solution)/shard_map/psum | solution.py:57
  64.3 3.4 copy-start.2
  69.0 1.9 copy-start
  79.0 322.0 %all-reduce.6.cloned.1.call-start = ((), (), s32[]{:S(2)}) async-start(), calls=%async_computation.2 | async-start | bytes 3145728 | tf_op jit(solution)/shard_map/psum | solution.py:62
  79.3 2.4 copy-start.3
  252.0 46.8 %copy-start.6 = (f32[512,512]{1,0:T(8,128)}, f32[512,512]{1,0:T(8,128)S(1)}, u32[]{:S(2)}) copy-start(f32[512,512]{1,0:T(8,128)S(1)} %get-tuple-element.92) | copy-start | bytes 3145732
  292.2 6.6 %copy-start.1 = (f32[2048,512]{1,0:T(8,128)S(1)}, f32[2048,512]{1,0:T(8,128)}, u32[]{:S(2)}) copy-start(f32[2048,512]{1,0:T(8,128)} %copy-done) | copy-start | bytes 12582916
  298.8 13.4 %slice-start = ((s8[6291456]{0:T(1024)(128)(4,1)}), s8[4194304]{0:T(1024)(128)(4,1)S(1)}, s32[]{:S(2)}) async-start(s8[6291456]{0:T(1024)(128)(4,1)} %bitcast.62), calls=%async_computation.3 | async-start | bytes 8388608
  303.4 8.7 %slice-start.1 = ((s8[6291456]{0:T(1024)(128)(4,1)}), s8[2097152]{0:T(1024)(128)(4,1)S(1)}, s32[]{:S(2)}) async-start(s8[6291456]{0:T(1024)(128)(4,1)} %bitcast.62), calls=%async_computation.4 | async-start | bytes 4194304
  311.2 1.0 copy-start.5
  401.0 23.9 %copy-start.4 = (f32[512,768]{1,0:T(8,128)S(1)}, f32[512,768]{1,0:T(8,128)}, u32[]{:S(2)}) copy-start(f32[512,768]{1,0:T(8,128)} %all-reduce.6.cloned.1.call-done) | copy-start | bytes 4718596
Sparse Core Ops, SparseCore 0:
  11.1 53.1 all-gather.3
  79.1 75.7 all-reduce.3
  323.9 77.1 all-reduce.5
where the time goes:
time: 441 us; the launch traced here: 433 us
  waiting for transfers between devices  174 us (39%)
  other arithmetic  124 us (28%)
  matrix products  74.6 us (17%)
  blocking collectives  24.6 us (6%)
  local copies, waits for them, and re-layouts  18.3 us (4%)
  between operations  17.1 us (4%)
    another operation x14, other arithmetic, orthonormal(): lower_factor = jnp.linalg.cholesky(gram_sum)  79 us
    psum x1, waiting for transfers between devices, shards(): coefficients = lax.psum(local_rows, 'row')  77.3 us
    psum x1, waiting for transfers between devices, shards(): gram_sum = lax.psum(local_gram, 'row')  68.5 us
    another operation x3, other arithmetic, orthonormal(): lax.linalg.triangular_solve(lower_factor, panel_cols.T, left_side=True, l...  40.3 us
    all_gather x1, waiting for transfers between devices, in_one_piece(): result = lax.all_gather(both, axis, axis=dim, tiled=True)  28.7 us
    all_gather x1, blocking collectives, picked(): lax.all_gather(array, axis)  24.6 us
    dot_general x1, matrix products, remove_span(): jnp.dot(basis_t.T, top_rows, precision=lax.Precision.HIGHEST, preferred_e...  23.9 us
    another operation x7, matrix products, orthonormal(): lax.linalg.triangular_solve(lower_factor, panel_cols.T, left_side=True, l...  18.9 us
  transfers between devices with their start and end apart: 3, of which 3 were waited for; matrix products, arithmetic and copies ran while one was open for 2% of the time, Pallas kernels for 0%

commit v1 on v0

--- a/solution.py
+++ b/solution.py
@@ -59,7 +59,8 @@
     local_rows = jnp.dot(
         basis_t, design, precision=lax.Precision.HIGHEST, preferred_element_type=jnp.float32
     )
-    coefficients = lax.psum(local_rows, "row")
+    d_next = lax.all_gather(local_rows, axis_name="row")
+    coefficients = jnp.sum(d_next, axis=0)
     residual = remove_span(design, basis_t, coefficients)
     return (coefficients, residual)
 

time: 441 us -> 502 us (1.14)
  waiting for transfers between devices: 174 us -> 229 us
  other arithmetic: 124 us -> 131 us
    all_gather x0 -> x1, waiting for transfers between devices: none -> 132 us  [shards(): d_next = lax.all_gather(local_rows, axis_name='row')]
    psum x1 -> x0, waiting for transfers between devices: 77.3 us -> none  [shards(): coefficients = lax.psum(local_rows, 'row')]
    reduce_sum x0 -> x1, other arithmetic: none -> 6.92 us  [shards(): coefficients = jnp.sum(d_next, axis=0)]
where the time goes in v1:
time: 502 us; the launch traced here: 493 us
  waiting for transfers between devices  229 us (46%)
  other arithmetic  131 us (26%)
  matrix products  74.2 us (15%)
  blocking collectives  24.6 us (5%)
  local copies, waits for them, and re-layouts  17.2 us (3%)
  between operations  16.9 us (3%)
    all_gather x1, waiting for transfers between devices, shards(): d_next = lax.all_gather(local_rows, axis_name='row')  132 us
    another operation x14, other arithmetic, orthonormal(): lower_factor = jnp.linalg.cholesky(gram_sum)  79 us
    psum x1, waiting for transfers between devices, shards(): gram_sum = lax.psum(local_gram, 'row')  68.3 us
    another operation x3, other arithmetic, orthonormal(): lax.linalg.triangular_solve(lower_factor, panel_cols.T, left_side=True, l...  40.3 us
    all_gather x1, waiting for transfers between devices, in_one_piece(): result = lax.all_gather(both, axis, axis=dim, tiled=True)  28.7 us
    all_gather x1, blocking collectives, picked(): lax.all_gather(array, axis)  24.6 us
    dot_general x1, matrix products, remove_span(): jnp.dot(basis_t.T, top_rows, precision=lax.Precision.HIGHEST, preferred_e...  23.5 us
    another operation x7, matrix products, orthonormal(): lax.linalg.triangular_solve(lower_factor, panel_cols.T, left_side=True, l...  18.8 us
  transfers between devices with their start and end apart: 3, of which 3 were waited for; matrix products, arithmetic and copies ran while one was open for 2% of the time, Pallas kernels for 0%

profile of v1, /device:TPU:2, one launch (start us, length us, event | category | flops | bytes accessed | tf_op | source)
XLA Modules:
  0.0 493.1 jit_solution(16940532252885069303)
XLA Ops:
  7.2 0.8 copy.12
  8.0 1.5 pad_maximum_fusion.3
  9.5 0.7 slice_bitcast_fusion.8
  10.2 24.6 %all-gather.2 = s32[32,2,512]{2,1,0:T(2,128)S(1)} all-gather(s32[1,2,512]{2,1,0:T(2,128)S(1)} %slice_bitcast_fusion.8), channel_id=2, replica_groups=mesh['row'=8,'col'=32] {'col'}, dimensions={0}, use_global_device_ids=true | all-gather | bytes 135168 | tf_op jit(solution)/shard_map/all_gather | solution.py:23
  34.8 0.8 slice_reduce_fusion
  35.6 28.7 %all-gather.6.cloned.1.call-done = bf16[2048,769]{1,0:T(8,128)(2,1)} async-done(((bf16[64,769]{1,0:T(8,128)(2,1)}), bf16[2048,769]{1,0:T(8,128)(2,1)}) %all-gather.6.cloned.1.call-update) | async-done | bytes 3149840 | tf_op jit(solution)/shard_map/all_gather | solution.py:15
  64.3 1.4 convert_reduce_fusion
  65.7 2.0 fusion.20
  67.7 1.3 multiply_multiply_fusion.1
  69.0 1.9 copy-done
  70.9 8.0 %fusion.49 = f32[512,512]{0,1:T(8,128)} fusion(f32[2048,512]{1,0:T(8,128)S(1)} %multiply_multiply_fusion.1), kind=kOutput, calls=%fused_computation.94 | convolution fusion | flops 6442450944 | bytes 5242880 | tf_op jit(solution)/shard_map/dot_general | solution.py:54
  79.5 2.4 fusion.18
  81.9 4.7 multiply_multiply_fusion
  86.6 68.3 %all-reduce.3.cloned.1.call-done = f32[512,512]{0,1:T(8,128)} async-done(((f32[512,512]{0,1:T(8,128)}), f32[512,512]{0,1:T(8,128)}) %all-reduce.3.cloned.1.call-update) | async-done | bytes 1048592 | tf_op jit(solution)/shard_map/psum | solution.py:57
  154.9 1.6 copy.14
  156.5 1.4 fusion.17
  158.0 11.7 %cholesky.104 = f32[128,128]{1,0:T(8,128)S(1)} custom-call(f32[128,128]{1,0:T(8,128)S(1)} %cholesky.266), custom_call_target="Cholesky" | custom-call | tf_op jit(solution)/shard_map/jit(cholesky)/cholesky | solution.py:39
  169.7 9.8 %custom-call.30 = f32[1,128,128]{1,2,0:T(8,128)S(1)} custom-call(f32[1,128,128]{2,1,0:T(8,128)S(1)} %get-tuple-element.33), custom_call_target="InvertDiagBlocksLowerTriangular" | custom-call | tf_op jit(solution)/shard_map/jit(cholesky)/cholesky | solution.py:39
  180.3 11.9 %cholesky.217 = f32[128,128]{1,0:T(8,128)S(1)} custom-call(f32[128,128]{1,0:T(8,128)S(1)} %cholesky.270), custom_call_target="Cholesky" | custom-call | tf_op jit(solution)/shard_map/jit(cholesky)/cholesky | solution.py:39
  192.2 9.8 %custom-call.31 = f32[1,128,128]{1,2,0:T(8,128)S(1)} custom-call(f32[1,128,128]{2,1,0:T(8,128)S(1)} %get-tuple-element.30), custom_call_target="InvertDiagBlocksLowerTriangular" | custom-call | tf_op jit(solution)/shard_map/jit(cholesky)/cholesky | solution.py:39
  202.7 11.7 %cholesky.238 = f32[128,128]{1,0:T(8,128)S(1)} custom-call(f32[128,128]{1,0:T(8,128)S(1)} %cholesky.275), custom_call_target="Cholesky" | custom-call | tf_op jit(solution)/shard_map/jit(cholesky)/cholesky | solution.py:39
  214.5 0.7 compare_reduce_fusion.1
  215.1 9.8 %custom-call.32 = f32[1,128,128]{1,2,0:T(8,128)S(1)} custom-call(f32[1,128,128]{2,1,0:T(8,128)S(1)} %get-tuple-element.27), custom_call_target="InvertDiagBlocksLowerTriangular" | custom-call | tf_op jit(solution)/shard_map/jit(cholesky)/cholesky | solution.py:39
  225.5 12.1 %cholesky.255 = f32[128,128]{1,0:T(8,128)S(1)} custom-call(f32[128,128]{1,0:T(8,128)S(1)} %convolution_subtract_fusion.5), custom_call_target="Cholesky" | custom-call | tf_op jit(solution)/shard_map/jit(cholesky)/cholesky | solution.py:39
  237.6 0.7 compare_reduce_fusion
  238.3 0.7 compare_reduce_fusion.2
  241.7 10.3 %while.1 = (s32[]{:T(128)}, f32[512,512]{1,0:T(8,128)S(1)}, s32[4,2]{0,1:T(2,128)S(1)}, f32[4,128,128]{2,1,0:T(8,128)}, s32[]{:T(128)}) while((s32[]{:T(128)}, f32[512,512]{1,0:T(8,128)S(1)}, s32[4,2]{0,1:T(2,128)S(1)}, f32[4,128,128]{2,1,0:T(8,128)}, s32[]{:T(128)}) %tuple.33), condition=%wide.while_cond, body=%wide.while_body.sunk | while | flops 2 | bytes 132205 | solution.py:40
  241.8 0.5 fusion.60
  242.4 2.0 bitcast_dynamic-update-slice_fusion.2
  244.4 0.5 fusion.60
  244.9 2.0 bitcast_dynamic-update-slice_fusion.2
  247.0 0.5 fusion.60
  247.5 2.0 bitcast_dynamic-update-slice_fusion.2
  249.6 0.5 fusion.60
  250.1 2.0 bitcast_dynamic-update-slice_fusion.2
  252.1 40.2 %custom-call.33 = f32[4,128,128]{1,2,0:T(8,128)S(1)} custom-call(f32[4,128,128]{2,1,0:T(8,128)} %get-tuple-element.9), custom_call_target="InvertDiagBlocksLowerTriangular" | custom-call | tf_op jit(solution)/shard_map/triangular_solve | solution.py:40
  292.2 2.4 fusion.15
  294.7 3.0 convolution_subtract_fusion.2
  297.7 1.1 fusion.37
  298.8 3.5 convolution_subtract_fusion.1
  302.4 1.1 fusion.35
  303.5 6.6 %fusion.6 = f32[128,2048]{0,1:T(8,128)S(1)} fusion(f32[128,2048]{1,0:T(8,128)S(1)} %fusion.35, f32[128,2048]{1,0:T(8,128)S(1)} %fusion.37, f32[128,2048]{1,0:T(8,128)S(1)} %fusion.15, f32[512,2048]{0,1:T(8,128)S(1)} %bitcast.62, f32[512,512]{1,0:T(8,128)} %copy-done.5), kind=kOutput, calls=%fused_computation.12 | convolution fusion | flops 1209794560 | bytes 5439488 | tf_op jit(solution)/shard_map/triangular_solve | solution.py:40
  310.1 1.1 fusion.34
  311.2 1.0 copy-done.4
  312.2 11.6 %fusion.9 = f32[512,768]{1,0:T(8,128)} fusion(f32[2048,768]{1,0:T(8,128)S(1)} %bitcast.64, f32[128,2048]{1,0:T(8,128)S(1)} %fusion.34, f32[128,2048]{1,0:T(8,128)S(1)} %fusion.35, f32[128,2048]{1,0:T(8,128)S(1)} %fusion.37, f32[128,2048]{1,0:T(8,128)S(1)} %fusion.15), kind=kOutput, calls=%fused_computation.15 | convolution fusion | flops 9666822144 | bytes 12058624 | tf_op jit(solution)/shard_map/dot_general | solution.py:59
  323.8 132.1 %all-gather.8.cloned.1.call-done = f32[4096,768]{1,0:T(8,128)} async-done(((f32[512,768]{1,0:T(8,128)}), f32[4096,768]{1,0:T(8,128)}) %all-gather.8.cloned.1.call-update) | async-done | bytes 12582928 | tf_op jit(solution)/shard_map/all_gather | solution.py:62
  455.9 6.9 %reduce_sum.9 = f32[512,768]{1,0:T(8,128)} reduce(f32[8,512,768]{2,1,0:T(8,128)} %bitcast.65, f32[]{:T(128)} %constant.143.clone.1), dimensions={0}, to_apply=%region_9.10 | reduce | flops 2752512 | bytes 14155780 | tf_op jit(solution)/shard_map/reduce_sum | solution.py:63
  462.8 23.5 %convolution_subtract_fusion = f32[2048,768]{1,0:T(8,128)} fusion(f32[2048,768]{1,0:T(8,128)} %multiply_multiply_fusion, f32[512,768]{1,0:T(8,128)} %reduce_sum.9, f32[128,2048]{1,0:T(8,128)} %copy-done.4, f32[128,2048]{1,0:T(8,128)S(1)} %fusion.35, f32[128,2048]{1,0:T(8,128)S(1)} %fusion.37, f32[128,2048]{1,0:T(8,128)S(1)} %fusion.15), kind=kOutput, calls=%fused_computation.5 | convolution fusion | flops 9668395008 | bytes 18350080 | tf_op jit(solution)/shard_map/dot_general | solution.py:44
  (44 shorter events, 3.3 us)
Async XLA Ops:
  7.2 57.1 %all-gather.6.cloned.1.call-start = ((), (), s32[]{:S(2)}) async-start(), calls=%async_computation | async-start | bytes 3784704 | tf_op jit(solution)/shard_map/all_gather | solution.py:15
  9.5 145.4 %all-reduce.3.cloned.1.call-start = ((), (), s32[]{:S(2)}) async-start(), calls=%async_computation.1 | async-start | bytes 2097152 | tf_op jit(solution)/shard_map/psum | solution.py:57
  64.3 3.4 copy-start.2
  69.0 1.9 copy-start
  79.0 376.9 %all-gather.8.cloned.1.call-start = ((), (), s32[]{:S(2)}) async-start(), calls=%async_computation.2 | async-start | bytes 14155776 | tf_op jit(solution)/shard_map/all_gather | solution.py:62
  79.5 2.4 copy-start.3
  252.1 46.8 %copy-start.5 = (f32[512,512]{1,0:T(8,128)}, f32[512,512]{1,0:T(8,128)S(1)}, u32[]{:S(2)}) copy-start(f32[512,512]{1,0:T(8,128)S(1)} %get-tuple-element.90) | copy-start | bytes 3145732
  292.2 6.6 %copy-start.1 = (f32[2048,512]{1,0:T(8,128)S(1)}, f32[2048,512]{1,0:T(8,128)}, u32[]{:S(2)}) copy-start(f32[2048,512]{1,0:T(8,128)} %copy-done) | copy-start | bytes 12582916
  298.8 13.4 %slice-start = ((s8[6291456]{0:T(1024)(128)(4,1)}), s8[4194304]{0:T(1024)(128)(4,1)S(1)}, s32[]{:S(2)}) async-start(s8[6291456]{0:T(1024)(128)(4,1)} %bitcast.63), calls=%async_computation.3 | async-start | bytes 8388608
  303.5 8.8 %slice-start.1 = ((s8[6291456]{0:T(1024)(128)(4,1)}), s8[2097152]{0:T(1024)(128)(4,1)S(1)}, s32[]{:S(2)}) async-start(s8[6291456]{0:T(1024)(128)(4,1)} %bitcast.63), calls=%async_computation.4 | async-start | bytes 4194304
  311.2 1.1 copy-start.4
Sparse Core Ops, SparseCore 0:
  11.1 53.1 all-gather.5
  79.1 75.7 all-reduce.2
  323.9 131.9 all-gather.7
